TPU v7x, 256 devices: a whole 4x4x8 slice. The times are simulated.
256 devices in a mesh: orb: 16 (over y, x), aux: 16 (over z, core).
Axes of the slice: x: 4, y: 4, z: 8, core: 2. Of those that a mesh axis runs over, the one named last changes fastest.
Arguments:
- b_rows: bfloat16 [4096, 128, 8, 128], P('aux', 'orb'), may hold values from -6 to 6
- col_blocks: int32 [16, 8], P('orb'), may hold values from 0 to 15, all different within a row
- g_occ: bfloat16 [2, 128, 128], P(None, 'orb'), may hold values from -0.5 to 0.5
- occ_live: int32 [2, 16, 16], replicated, may hold values 0 or 1
- g_virt: bfloat16 [2, 16, 128, 128], P(None, 'orb', 'aux'), may hold values from -0.5 to 0.5
- tau_weight: float32 [2], replicated, may hold values from 0.5 to 2
Outputs:
- chi: float32 [256, 4096], P('orb', 'aux')
Inputs may be any that keep to these rules, and one draw needn't show every extreme that they name: `col_blocks`: each row group lists 8 different column blocks, and every column block is listed by some row group.
All inputs are finite; a program needn't handle non-finite values.
Results may differ from a plain program's by a relative error of at most 0.0041.
Values may be sent and summed in bfloat16 or wider, within the bound.
A program may use at most 128 MiB of HBM per device.

v0:
```python
import math
import jax
import jax.numpy as jnp
from jax import lax
from jax.sharding import PartitionSpec as P


def on_device(b_rows, col_blocks, g_occ, occ_live, g_virt, tau_weight):
    orb_count = lax.axis_size("orb")
    aux_dev, rows_dev, slot_count, tile_width = b_rows.shape
    tau_count = g_occ.shape[0]
    picked = (col_blocks[0][:, None] == jnp.arange(orb_count, dtype=jnp.int32)[None, :]).astype(
        jnp.bfloat16
    )
    outgoing = jnp.einsum("prkc,kd->prdc", b_rows, picked)
    occ_full = lax.all_gather(g_occ, "orb", axis=1, tiled=True)
    total_rows = occ_full.shape[1]
    live_mask = jnp.repeat(jnp.repeat(occ_live, rows_dev, axis=1), rows_dev, axis=2).astype(
        jnp.bfloat16
    )
    occ_masked = occ_full * live_mask
    virt_block = lax.all_gather(g_virt, "aux", axis=2, tiled=True)
    col_dense = lax.all_to_all(outgoing, "orb", split_axis=2, concat_axis=1, tiled=True).reshape(
        aux_dev, total_rows, tile_width
    )
    virt_list = []
    for moment in range(tau_count):
        product = jnp.dot(
            col_dense.reshape(aux_dev * total_rows, tile_width),
            virt_block[moment, 0],
            preferred_element_type=jnp.float32,
        )
        virt_list.append(product.astype(jnp.bfloat16).reshape(aux_dev, total_rows, tile_width))
    partial_value = jnp.zeros((aux_dev, aux_dev), jnp.float32)
    for moment in range(tau_count):
        occ_prod = jnp.einsum(
            "mn,qnc->qmc", occ_masked[moment], col_dense, preferred_element_type=jnp.float32
        ).astype(jnp.bfloat16)
        term = jnp.einsum(
            "pmc,qmc->qp", virt_list[moment], occ_prod, preferred_element_type=jnp.float32
        )
        partial_value = partial_value + tau_weight[moment] * term
    partial_value = partial_value * (1.0 / math.sqrt(total_rows * tile_width * orb_count))
    whole_sum = lax.psum(partial_value, "orb")
    share_rows = aux_dev // orb_count
    share = lax.dynamic_slice_in_dim(whole_sum, lax.axis_index("orb") * share_rows, share_rows, 0)
    return share


def solution(mesh):
    in_specs = (
        P("aux", "orb", None, None),
        P("orb", None),
        P(None, "orb", None),
        P(),
        P(None, "orb", "aux", None),
        P(),
    )
    out_specs = P("orb", "aux")
    return jax.shard_map(
        on_device, mesh=mesh, in_specs=in_specs, out_specs=out_specs, check_vma=False
    )
```

profile of v0, /device:TPU:2, one launch (start us, length us, event | category | flops | bytes accessed | tf_op | source)
XLA Modules:
  0.0 368.9 jit_solution(9843376873879229038)
XLA Ops:
  6.5 6.3 %convolution_bitcast_fusion = bf16[256,8,16,128]{3,2,1,0:T(8,128)(2,1)} fusion(bf16[256,8,8,128]{3,2,1,0:T(8,128)(2,1)} %param.6, s32[8]{0:T(128)} %bitcast.83), kind=kOutput, calls=%fused_computation.8 | convolution fusion | flops 67108992 | bytes 12582944 | tf_op jit(solution)/shard_map/prkc,kd->prdc/dot_general | solution.py:15
  12.8 8.8 %copy.23 = bf16[256,8,16,128]{3,1,0,2:T(8,128)(2,1)} copy(bf16[256,8,16,128]{3,2,1,0:T(8,128)(2,1)} %convolution_bitcast_fusion) | data formatting | bytes 16777216 | tf_op jit(solution)/shard_map/prkc,kd->prdc/transpose | solution.py:15
  21.6 0.0 copy-start.1
  21.6 0.0 copy-start.2
  21.6 0.0 copy-start.3
  21.6 0.0 copy-start.4
  21.6 7.6 %all-to-all-start = ((bf16[256,8,16,128]{3,1,0,2:T(8,128)(2,1)}), bf16[256,8,16,128]{3,1,0,2:T(8,128)(2,1)}, u32[]{:S(2)}, u32[]{:S(2)}) async-start(bf16[256,8,16,128]{3,1,0,2:T(8,128)(2,1)} %copy.23), calls=%async_computation | async-start | bytes 16777216 | tf_op jit(solution)/shard_map/all_to_all | solution.py:23
  29.2 0.0 all-reduce.2.cloned.1.call-start
  29.3 0.0 copy-done.1
  29.3 0.1 copy.25
  29.4 0.1 copy.26
  29.5 0.0 copy-done.2
  29.5 137.6 %all_gather.6 = bf16[2,128,128]{2,1,0:T(8,128)(2,1)S(1)} all-gather(bf16[2,8,128]{2,1,0:T(8,128)(2,1)S(1)} %copy-done.2), channel_id=1, replica_groups=mesh['orb'=16,'aux'=16] {'orb'}, dimensions={1}, use_global_device_ids=true | all-gather | bytes 69632 | tf_op jit(solution)/shard_map/all_gather | solution.py:16
  167.1 0.0 copy-done.3
  167.2 20.1 %all_gather.7 = bf16[2,1,128,128]{3,2,1,0:T(8,128)(2,1)S(1)} all-gather(bf16[2,1,8,128]{3,2,1,0:T(8,128)(2,1)S(1)} %copy-done.3), channel_id=1, replica_groups=mesh['orb'=16,'aux'=16] {'aux'}, dimensions={2}, use_global_device_ids=true | all-gather | bytes 69632 | tf_op jit(solution)/shard_map/all_gather | solution.py:22
  187.3 0.0 copy-done.4
  187.3 0.6 fusion.31
  187.9 0.0 all-to-all-done
  187.9 9.0 %copy.34 = bf16[256,8,16,128]{3,1,2,0:T(8,128)(2,1)} copy(bf16[256,8,16,128]{3,1,0,2:T(8,128)(2,1)} %all-to-all-done) | data formatting | bytes 16777216 | tf_op jit(solution)/shard_map/all_to_all | solution.py:23
  196.9 0.0 copy-start
  196.9 9.1 %convolution_convert_fusion = bf16[32768,128]{1,0:T(8,128)(2,1)} fusion(bf16[32768,128]{1,0:T(8,128)(2,1)} %bitcast.78, bf16[2,1,128,128]{3,2,1,0:T(8,128)(2,1)S(1)} %all_gather.7), kind=kOutput, calls=%fused_computation | convolution fusion | flops 1077936128 | bytes 16809984 | tf_op jit(solution)/shard_map/dot_general | solution.py:28
  206.0 0.0 copy-done
  206.0 4.5 %convolution_convert_fusion.1 = bf16[32768,128]{1,0:T(8,128)(2,1)} fusion(bf16[32768,128]{1,0:T(8,128)(2,1)S(1)} %bitcast.80, bf16[2,1,128,128]{3,2,1,0:T(8,128)(2,1)S(1)} %all_gather.7), kind=kOutput, calls=%fused_computation.1 | convolution fusion | flops 1077936128 | bytes 16809984 | tf_op jit(solution)/shard_map/dot_general | solution.py:28
  210.5 11.8 %copy.30 = bf16[256,128,128]{1,0,2:T(8,128)(2,1)} copy(bf16[256,128,128]{2,1,0:T(8,128)(2,1)} %bitcast.82) | data formatting | bytes 16777216 | tf_op jit(solution)/shard_map/reshape | solution.py:33
  222.3 11.8 %copy.27 = bf16[256,128,128]{1,0,2:T(8,128)(2,1)} copy(bf16[256,128,128]{2,1,0:T(8,128)(2,1)} %bitcast.79) | data formatting | bytes 16777216 | tf_op jit(solution)/shard_map/reshape | solution.py:23
  234.1 12.3 %copy.28 = bf16[256,128,128]{1,0,2:T(8,128)(2,1)} copy(bf16[256,128,128]{2,1,0:T(8,128)(2,1)} %bitcast.81) | data formatting | bytes 16777216 | tf_op jit(solution)/shard_map/reshape | solution.py:33
  246.4 11.0 %fusion.16 = f32[256,256]{1,0:T(8,128)S(1)} fusion(bf16[256,128,128]{1,0,2:T(8,128)(2,1)} %copy.30, bf16[256,128,128]{1,0,2:T(8,128)(2,1)} %copy.27, f32[]{:T(128)} %bitcast.18, bf16[2,128,128]{2,1,0:T(8,128)(2,1)S(1)} %mul.25), kind=kOutput, calls=%fused_computation.13 | convolution fusion | flops 3225485312 | bytes 17072132 | tf_op jit(solution)/shard_map/pmc,qmc->qp/dot_general | solution.py:39
  257.5 11.8 %fusion.25 = f32[256,256]{1,0:T(8,128)} fusion(f32[256,256]{1,0:T(8,128)S(1)} %fusion.16, bf16[256,128,128]{1,0,2:T(8,128)(2,1)} %copy.28, bf16[256,128,128]{1,0,2:T(8,128)(2,1)} %copy.27, f32[]{:T(128)} %bitcast, bf16[2,128,128]{2,1,0:T(8,128)(2,1)S(1)} %mul.25), kind=kOutput, calls=%fused_computation.16 | convolution fusion | flops 3225616384 | bytes 17334276 | tf_op jit(solution)/shard_map/pmc,qmc->qp/dot_general | solution.py:39
  269.3 0.0 all-reduce.2.cloned.1.call-update
  269.3 91.4 %all-reduce.2.cloned.1.call-done = f32[256,256]{1,0:T(8,128)} async-done(((f32[256,256]{1,0:T(8,128)}), f32[256,256]{1,0:T(8,128)}) %all-reduce.2.cloned.1.call-update) | async-done | bytes 262160 | tf_op jit(solution)/shard_map/psum | solution.py:44
  360.7 1.3 constant_dynamic-slice_fusion
  (4 shorter events, 0.1 us)
Async XLA Ops:
  21.6 7.7 %copy-start.1 = (s32[2,16,16]{2,1,0:T(8,128)S(1)}, s32[2,16,16]{2,1,0:T(8,128)}, u32[]{:S(2)}) copy-start(s32[2,16,16]{2,1,0:T(8,128)} %param.9) | copy-start | bytes 6148
  21.6 8.0 %copy-start.2 = (bf16[2,8,128]{2,1,0:T(8,128)(2,1)S(1)}, bf16[2,8,128]{2,1,0:T(8,128)(2,1)}, u32[]{:S(2)}) copy-start(bf16[2,8,128]{2,1,0:T(8,128)(2,1)} %param.8) | copy-start | bytes 12292
  21.6 145.6 %copy-start.3 = (bf16[2,1,8,128]{3,2,1,0:T(8,128)(2,1)S(1)}, bf16[2,1,8,128]{3,2,1,0:T(8,128)(2,1)}, u32[]{:S(2)}) copy-start(bf16[2,1,8,128]{3,2,1,0:T(8,128)(2,1)} %param.10) | copy-start | bytes 12292
  21.6 165.7 %copy-start.4 = (f32[2]{0:T(128)S(1)}, f32[2]{0:T(128)}, u32[]{:S(2)}) copy-start(f32[2]{0:T(128)} %param.11) | copy-start | bytes 28
  21.6 166.3 %all-to-all-start = ((bf16[256,8,16,128]{3,1,0,2:T(8,128)(2,1)}), bf16[256,8,16,128]{3,1,0,2:T(8,128)(2,1)}, u32[]{:S(2)}, u32[]{:S(2)}) async-start(bf16[256,8,16,128]{3,1,0,2:T(8,128)(2,1)} %copy.23), calls=%async_computation | async-start | bytes 16777216 | tf_op jit(solution)/shard_map/all_to_all | solution.py:23
  29.2 331.5 %all-reduce.2.cloned.1.call-start = ((), (), s32[]{:S(2)}) async-start(), calls=%async_computation.1 | async-start | bytes 524288 | tf_op jit(solution)/shard_map/psum | solution.py:44
  196.9 9.1 %copy-start = (bf16[256,8,16,128]{3,1,2,0:T(8,128)(2,1)S(1)}, bf16[256,8,16,128]{3,1,2,0:T(8,128)(2,1)}, u32[]{:S(2)}) copy-start(bf16[256,8,16,128]{3,1,2,0:T(8,128)(2,1)} %copy.34) | copy-start | bytes 25165828
Sparse Core Ops, SparseCore 0:
  269.4 91.2 all-reduce.1
where the time goes:
time: 370 us; the launch traced here: 369 us
  blocking collectives  158 us (43%)
  waiting for transfers between devices  91.4 us (25%)
  local copies, waits for them, and re-layouts  55.9 us (15%)
  matrix products  42.7 us (12%)
  between operations  13.5 us (4%)
  starting transfers between devices  7.66 us (2%)
    all_gather x1, blocking collectives, on_device(): occ_full = lax.all_gather(g_occ, 'orb', axis=1, tiled=True)  138 us
    psum x1, waiting for transfers between devices, on_device(): whole_sum = lax.psum(partial_value, 'orb')  91.4 us
    reshape x2, local copies, waits for them, and re-layouts, on_device(): product.astype(jnp.bfloat16).reshape(aux_dev, total_rows, tile_width)  24.1 us
    dot_general x2, matrix products, on_device(): jnp.einsum('pmc,qmc->qp', virt_list[moment], occ_prod, preferred_element_...  22.9 us
    all_gather x1, blocking collectives, on_device(): virt_block = lax.all_gather(g_virt, 'aux', axis=2, tiled=True)  20.1 us
    dot_general x2, matrix products, on_device(): jnp.dot(col_dense.reshape(aux_dev * total_rows, tile_width), virt_block[m...  13.6 us
    reshape x1, local copies, waits for them, and re-layouts, on_device(): lax.all_to_all(outgoing, 'orb', split_axis=2, concat_axis=1, tiled=True)  11.8 us
    all_to_all x1, local copies, waits for them, and re-layouts, on_device(): lax.all_to_all(outgoing, 'orb', split_axis=2, concat_axis=1, tiled=True)  9.03 us
  transfers between devices with their start and end apart: 2, of which 1 were waited for; matrix products, arithmetic and copies ran while one was open for 0% of the time, Pallas kernels for 0%

commit v1 on v0

--- a/solution.py
+++ b/solution.py
@@ -41,7 +41,11 @@
         )
         partial_value = partial_value + tau_weight[moment] * term
     partial_value = partial_value * (1.0 / math.sqrt(total_rows * tile_width * orb_count))
-    whole_sum = lax.psum(partial_value, "orb")
+    whole_sum = partial_value
+    for hop in (1, 2, 4, 8):
+        whole_sum = whole_sum + lax.ppermute(
+            whole_sum, "orb", [(dev, dev ^ hop) for dev in range(16)]
+        )
     share_rows = aux_dev // orb_count
     share = lax.dynamic_slice_in_dim(whole_sum, lax.axis_index("orb") * share_rows, share_rows, 0)
     return share

time: 370 us -> 296 us (0.80)
  waiting for transfers between devices: 91.4 us -> 25.8 us
  between operations: 13.5 us -> 0.1 us
  starting transfers between devices: 7.66 us -> 14.6 us
    psum x1 -> x0, waiting for transfers between devices: 91.4 us -> none  [on_device(): whole_sum = lax.psum(partial_value, 'orb')]
    ppermute x0 -> x4, waiting for transfers between devices: none -> 25.8 us  [on_device(): lax.ppermute(whole_sum, 'orb', [(dev, dev ^ hop) for dev in range(16)])]
    ppermute x0 -> x4, starting transfers between devices: none -> 7.03 us  [on_device(): lax.ppermute(whole_sum, 'orb', [(dev, dev ^ hop) for dev in range(16)])]
  transfers between devices with their start and end apart: 2 -> 5, of which waited for: 1 -> 4; matrix products, arithmetic and copies ran while one was open for 0% -> 0% of each run, Pallas kernels for 0% -> 0%
where the time goes in v1:
time: 296 us; the launch traced here: 295 us
  blocking collectives  158 us (53%)
  local copies, waits for them, and re-layouts  53.9 us (18%)
  matrix products  41.9 us (14%)
  waiting for transfers between devices  25.8 us (9%)
  starting transfers between devices  14.6 us (5%)
    all_gather x1, blocking collectives, on_device(): occ_full = lax.all_gather(g_occ, 'orb', axis=1, tiled=True)  138 us
    ppermute x4, waiting for transfers between devices, on_device(): lax.ppermute(whole_sum, 'orb', [(dev, dev ^ hop) for dev in range(16)])  25.8 us
    reshape x2, local copies, waits for them, and re-layouts, on_device(): product.astype(jnp.bfloat16).reshape(aux_dev, total_rows, tile_width)  23.6 us
    dot_general x2, matrix products, on_device(): jnp.einsum('pmc,qmc->qp', virt_list[moment], occ_prod, preferred_element_...  22.1 us
    all_gather x1, blocking collectives, on_device(): virt_block = lax.all_gather(g_virt, 'aux', axis=2, tiled=True)  20.1 us
    dot_general x2, matrix products, on_device(): jnp.dot(col_dense.reshape(aux_dev * total_rows, tile_width), virt_block[m...  13.5 us
    reshape x1, local copies, waits for them, and re-layouts, on_device(): lax.all_to_all(outgoing, 'orb', split_axis=2, concat_axis=1, tiled=True)  11.7 us
    all_to_all x1, local copies, waits for them, and re-layouts, on_device(): lax.all_to_all(outgoing, 'orb', split_axis=2, concat_axis=1, tiled=True)  9.01 us
  transfers between devices with their start and end apart: 5, of which 4 were waited for; matrix products, arithmetic and copies ran while one was open for 0% of the time, Pallas kernels for 0%

profile of v1, /device:TPU:2, one launch (start us, length us, event | category | flops | bytes accessed | tf_op | source)
XLA Modules:
  0.0 294.9 jit_solution(8986897087281383094)
XLA Ops:
  0.0 6.3 %convolution_bitcast_fusion = bf16[256,8,16,128]{3,2,1,0:T(8,128)(2,1)} fusion(bf16[256,8,8,128]{3,2,1,0:T(8,128)(2,1)} %param.6, s32[8]{0:T(128)} %bitcast.83), kind=kOutput, calls=%fused_computation.8 | convolution fusion | flops 67108992 | bytes 12582944 | tf_op jit(solution)/shard_map/prkc,kd->prdc/dot_general | solution.py:15
  6.3 8.8 %copy.23 = bf16[256,8,16,128]{3,1,0,2:T(8,128)(2,1)} copy(bf16[256,8,16,128]{3,2,1,0:T(8,128)(2,1)} %convolution_bitcast_fusion) | data formatting | bytes 16777216 | tf_op jit(solution)/shard_map/prkc,kd->prdc/transpose | solution.py:15
  15.0 0.0 copy-start.1
  15.0 7.6 %all-to-all-start = ((bf16[256,8,16,128]{3,1,0,2:T(8,128)(2,1)}), bf16[256,8,16,128]{3,1,0,2:T(8,128)(2,1)}, u32[]{:S(2)}, u32[]{:S(2)}) async-start(bf16[256,8,16,128]{3,1,0,2:T(8,128)(2,1)} %copy.23), calls=%async_computation | async-start | bytes 16777216 | tf_op jit(solution)/shard_map/all_to_all | solution.py:23
  22.6 0.0 copy-done.1
  22.7 0.1 copy.25
  22.8 0.1 copy.26
  22.9 0.0 copy-done.2
  22.9 137.6 %all_gather.6 = bf16[2,128,128]{2,1,0:T(8,128)(2,1)S(1)} all-gather(bf16[2,8,128]{2,1,0:T(8,128)(2,1)S(1)} %copy-done.2), channel_id=1, replica_groups=mesh['orb'=16,'aux'=16] {'orb'}, dimensions={1}, use_global_device_ids=true | all-gather | bytes 69632 | tf_op jit(solution)/shard_map/all_gather | solution.py:16
  160.6 0.0 copy-done.3
  160.6 20.1 %all_gather.7 = bf16[2,1,128,128]{3,2,1,0:T(8,128)(2,1)S(1)} all-gather(bf16[2,1,8,128]{3,2,1,0:T(8,128)(2,1)S(1)} %copy-done.3), channel_id=1, replica_groups=mesh['orb'=16,'aux'=16] {'aux'}, dimensions={2}, use_global_device_ids=true | all-gather | bytes 69632 | tf_op jit(solution)/shard_map/all_gather | solution.py:22
  180.7 0.0 copy-done.4
  180.8 0.6 fusion.31
  181.3 0.0 all-to-all-done
  181.3 9.0 %copy.34 = bf16[256,8,16,128]{3,1,2,0:T(8,128)(2,1)} copy(bf16[256,8,16,128]{3,1,0,2:T(8,128)(2,1)} %all-to-all-done) | data formatting | bytes 16777216 | tf_op jit(solution)/shard_map/all_to_all | solution.py:23
  190.4 9.1 %convolution_convert_fusion = bf16[32768,128]{1,0:T(8,128)(2,1)} fusion(bf16[32768,128]{1,0:T(8,128)(2,1)} %bitcast.78, bf16[2,1,128,128]{3,2,1,0:T(8,128)(2,1)S(1)} %all_gather.7), kind=kOutput, calls=%fused_computation | convolution fusion | flops 1077936128 | bytes 16809984 | tf_op jit(solution)/shard_map/dot_general | solution.py:28
  199.4 0.0 copy-done
  199.4 4.5 %convolution_convert_fusion.1 = bf16[32768,128]{1,0:T(8,128)(2,1)} fusion(bf16[32768,128]{1,0:T(8,128)(2,1)S(1)} %bitcast.80, bf16[2,1,128,128]{3,2,1,0:T(8,128)(2,1)S(1)} %all_gather.7), kind=kOutput, calls=%fused_computation.1 | convolution fusion | flops 1077936128 | bytes 16809984 | tf_op jit(solution)/shard_map/dot_general | solution.py:28
  203.9 11.8 %copy.30 = bf16[256,128,128]{1,0,2:T(8,128)(2,1)} copy(bf16[256,128,128]{2,1,0:T(8,128)(2,1)} %bitcast.82) | data formatting | bytes 16777216 | tf_op jit(solution)/shard_map/reshape | solution.py:33
  215.7 11.7 %copy.27 = bf16[256,128,128]{1,0,2:T(8,128)(2,1)} copy(bf16[256,128,128]{2,1,0:T(8,128)(2,1)} %bitcast.79) | data formatting | bytes 16777216 | tf_op jit(solution)/shard_map/reshape | solution.py:23
  227.5 11.8 %copy.28 = bf16[256,128,128]{1,0,2:T(8,128)(2,1)} copy(bf16[256,128,128]{2,1,0:T(8,128)(2,1)} %bitcast.81) | data formatting | bytes 16777216 | tf_op jit(solution)/shard_map/reshape | solution.py:33
  239.2 11.0 %fusion.16 = f32[256,256]{1,0:T(8,128)S(1)} fusion(bf16[256,128,128]{1,0,2:T(8,128)(2,1)} %copy.30, bf16[256,128,128]{1,0,2:T(8,128)(2,1)} %copy.27, f32[]{:T(128)} %bitcast.18, bf16[2,128,128]{2,1,0:T(8,128)(2,1)S(1)} %mul.25), kind=kOutput, calls=%fused_computation.13 | convolution fusion | flops 3225485312 | bytes 17072132 | tf_op jit(solution)/shard_map/pmc,qmc->qp/dot_general | solution.py:39
  250.2 11.1 %fusion.25 = f32[256,256]{1,0:T(8,128)S(1)} fusion(f32[256,256]{1,0:T(8,128)S(1)} %fusion.16, bf16[256,128,128]{1,0,2:T(8,128)(2,1)} %copy.28, bf16[256,128,128]{1,0,2:T(8,128)(2,1)} %copy.27, f32[]{:T(128)} %bitcast, bf16[2,128,128]{2,1,0:T(8,128)(2,1)S(1)} %mul.25), kind=kOutput, calls=%fused_computation.16 | convolution fusion | flops 3225616384 | bytes 17334276 | tf_op jit(solution)/shard_map/pmc,qmc->qp/dot_general | solution.py:39
  261.3 0.8 collective-permute-start
  262.2 7.8 %collective-permute-done = f32[256,256]{1,0:T(8,128)S(1)} collective-permute-done((f32[256,256]{1,0:T(8,128)S(1)}, f32[256,256]{1,0:T(8,128)S(1)}, u32[]{:S(2)}, u32[]{:S(2)}) %collective-permute-start) | collective-permute-done | bytes 262176 | tf_op jit(solution)/shard_map/ppermute | solution.py:46
  270.0 2.2 collective-permute-start.1
  272.1 7.2 %collective-permute-done.1 = f32[256,256]{1,0:T(8,128)S(1)} collective-permute-done((f32[256,256]{1,0:T(8,128)S(1)}, f32[256,256]{1,0:T(8,128)S(1)}, u32[]{:S(2)}, u32[]{:S(2)}) %collective-permute-start.1) | collective-permute-done | bytes 262176 | tf_op jit(solution)/shard_map/ppermute | solution.py:46
  279.4 1.3 collective-permute-start.2
  280.6 5.6 %collective-permute-done.2 = f32[256,256]{1,0:T(8,128)S(1)} collective-permute-done((f32[256,256]{1,0:T(8,128)S(1)}, f32[256,256]{1,0:T(8,128)S(1)}, u32[]{:S(2)}, u32[]{:S(2)}) %collective-permute-start.2) | collective-permute-done | bytes 262176 | tf_op jit(solution)/shard_map/ppermute | solution.py:46
  286.3 2.8 collective-permute-start.3
  289.1 5.2 %collective-permute-done.3 = f32[256,256]{1,0:T(8,128)S(1)} collective-permute-done((f32[256,256]{1,0:T(8,128)S(1)}, f32[256,256]{1,0:T(8,128)S(1)}, u32[]{:S(2)}, u32[]{:S(2)}) %collective-permute-start.3) | collective-permute-done | bytes 262176 | tf_op jit(solution)/shard_map/ppermute | solution.py:46
  294.3 0.6 dynamic-slice_add_fusion
  (11 shorter events, 0.2 us)
Async XLA Ops:
  15.0 7.6 %copy-start.1 = (s32[2,16,16]{2,1,0:T(8,128)S(1)}, s32[2,16,16]{2,1,0:T(8,128)}, u32[]{:S(2)}) copy-start(s32[2,16,16]{2,1,0:T(8,128)} %param.9) | copy-start | bytes 6148
  15.0 7.9 %copy-start.2 = (bf16[2,8,128]{2,1,0:T(8,128)(2,1)S(1)}, bf16[2,8,128]{2,1,0:T(8,128)(2,1)}, u32[]{:S(2)}) copy-start(bf16[2,8,128]{2,1,0:T(8,128)(2,1)} %param.8) | copy-start | bytes 12292
  15.0 145.6 %copy-start.3 = (bf16[2,1,8,128]{3,2,1,0:T(8,128)(2,1)S(1)}, bf16[2,1,8,128]{3,2,1,0:T(8,128)(2,1)}, u32[]{:S(2)}) copy-start(bf16[2,1,8,128]{3,2,1,0:T(8,128)(2,1)} %param.10) | copy-start | bytes 12292
  15.0 165.7 %copy-start.4 = (f32[2]{0:T(128)S(1)}, f32[2]{0:T(128)}, u32[]{:S(2)}) copy-start(f32[2]{0:T(128)} %param.11) | copy-start | bytes 28
  15.0 166.3 %all-to-all-start = ((bf16[256,8,16,128]{3,1,0,2:T(8,128)(2,1)}), bf16[256,8,16,128]{3,1,0,2:T(8,128)(2,1)}, u32[]{:S(2)}, u32[]{:S(2)}) async-start(bf16[256,8,16,128]{3,1,0,2:T(8,128)(2,1)} %copy.23), calls=%async_computation | async-start | bytes 16777216 | tf_op jit(solution)/shard_map/all_to_all | solution.py:23
  190.4 9.1 %copy-start = (bf16[256,8,16,128]{3,1,2,0:T(8,128)(2,1)S(1)}, bf16[256,8,16,128]{3,1,2,0:T(8,128)(2,1)}, u32[]{:S(2)}) copy-start(bf16[256,8,16,128]{3,1,2,0:T(8,128)(2,1)} %copy.34) | copy-start | bytes 25165828
  261.3 8.6 %collective-permute-start = (f32[256,256]{1,0:T(8,128)S(1)}, f32[256,256]{1,0:T(8,128)S(1)}, u32[]{:S(2)}, u32[]{:S(2)}) collective-permute-start(f32[256,256]{1,0:T(8,128)S(1)} %fusion.25), channel_id=1, source_target_pairs={{0,16},{16,0},{32,48},{48,32},{64,80},{80,64},{96,112},{112,96},{1... | collective-permute-start | bytes 786440 | tf_op jit(solution)/shard_map/ppermute | solution.py:46
  270.0 9.3 %collective-permute-start.1 = (f32[256,256]{1,0:T(8,128)S(1)}, f32[256,256]{1,0:T(8,128)S(1)}, u32[]{:S(2)}, u32[]{:S(2)}) collective-permute-start(f32[256,256]{1,0:T(8,128)S(1)} %add.19), channel_id=1, source_target_pairs={{0,32},{16,48},{32,0},{48,16},{64,96},{80,112},{96,64},{112,80},{1... | collective-permute-start | bytes 786440 | tf_op jit(solution)/shard_map/ppermute | solution.py:46
  279.4 6.9 %collective-permute-start.2 = (f32[256,256]{1,0:T(8,128)S(1)}, f32[256,256]{1,0:T(8,128)S(1)}, u32[]{:S(2)}, u32[]{:S(2)}) collective-permute-start(f32[256,256]{1,0:T(8,128)S(1)} %add.20), channel_id=1, source_target_pairs={{0,64},{16,80},{32,96},{48,112},{64,0},{80,16},{96,32},{112,48},{1... | collective-permute-start | bytes 786440 | tf_op jit(solution)/shard_map/ppermute | solution.py:46
  286.3 8.0 %collective-permute-start.3 = (f32[256,256]{1,0:T(8,128)S(1)}, f32[256,256]{1,0:T(8,128)S(1)}, u32[]{:S(2)}, u32[]{:S(2)}) collective-permute-start(f32[256,256]{1,0:T(8,128)S(1)} %add.21), channel_id=1, source_target_pairs={{0,128},{16,144},{32,160},{48,176},{64,192},{80,208},{96,224},{112... | collective-permute-start | bytes 786440 | tf_op jit(solution)/shard_map/ppermute | solution.py:46
